TPU v7x, 32 devices: a whole 2x2x4 slice. The times are simulated.
32 devices in a mesh: grp: 4 (over x, core), dev: 8 (over z, y).
Axes of the slice: x: 2, y: 2, z: 4, core: 2. Of those that a mesh axis runs over, the one named last changes fastest.
Arguments:
- positions: float32 [3, 32768], P(None, ('grp', 'dev')), may hold values from -6 to 6
- rotations: float32 [9, 32768], P(None, ('grp', 'dev')), may hold values from -1 to 1, as said below
- clump_kind: int32 [32768], P(('grp', 'dev')), may hold values from 0 to 7
- sub_offsets: int32 [8, 3, 64], replicated, may hold values from -8 to 8
- pair_blocks: int32 [2, 32768], P(None, ('grp', 'dev')), may hold values from 0 to 16383, as said below
- pair_count: int32 [32], P(('grp', 'dev')), may hold values from 1 to 1024, as said below
Outputs:
- clump_force: float32 [3, 32768], P(None, ('grp', 'dev'))
- clump_torque: float32 [3, 32768], P(None, ('grp', 'dev'))
Inputs may be any that keep to these rules, and one draw needn't show every extreme that they name: `rotations`: each column is a proper rotation matrix in row-major order. `pair_blocks`: the two blocks of a slot differ. A slot on a device of group g names as its first block one of group g's blocks (g * 4096 to (g + 1) * 4096 - 1) and as its second one of group g's blocks or of the 128 nearest blocks of groups g - 1 and g + 1, that is a block from g * 4096 - 128 to (g + 1) * 4096 + 127. `pair_count`: each device has at least one live slot.
All inputs are finite; a program needn't handle non-finite values.
Results may differ from a plain program's by a relative error of at most 0.0003.
Values sent between devices are 32-bit elements; how exact they have to be, the bound alone decides.
No kernel may reach another device: no remote copies, remote signals or barrier semaphores. Data moves between devices by JAX's collectives and lax.ppermute only.
A program may use at most 128 MiB of HBM per device.

v0:
```python
import jax
import jax.numpy as jnp
from jax import lax
from jax.sharding import PartitionSpec as P

RIM = 128
OFFSET_UNIT = 0.125
REACH_SQUARED = 4.0
STIFFNESS = 1.0 / 256.0


def padded(cells, sides, width):
    for axis, dim in sides:
        count = lax.axis_size(axis)
        ends = count - 1
        head = lax.slice_in_dim(cells, 0, width, axis=dim)
        tail = lax.slice_in_dim(cells, cells.shape[dim] - width, cells.shape[dim], axis=dim)
        cells = jnp.concatenate(
            [
                lax.ppermute(tail, axis, [(i, (i + 1) % count) for i in range(ends)]),
                cells,
                lax.ppermute(head, axis, [((i + 1) % count, i) for i in range(ends)]),
            ],
            axis=dim,
        )
    return cells


def cross_axis(left_vec, right_vec):
    return jnp.stack(
        [
            left_vec[1] * right_vec[2] - left_vec[2] * right_vec[1],
            left_vec[2] * right_vec[0] - left_vec[0] * right_vec[2],
            left_vec[0] * right_vec[1] - left_vec[1] * right_vec[0],
        ],
        0,
    )


def place_blocks(centers, rotation_rows, onehot, offset_table):
    sub_count = offset_table.shape[1] // 3
    offsets = jnp.dot(onehot, offset_table, precision=lax.Precision.HIGHEST).reshape(
        -1, 3, sub_count
    )
    rotation_mats = rotation_rows.T.reshape(-1, 3, 3)
    world_pos = centers.T[:, :, None] + jnp.einsum(
        "ckm,cms->cks", rotation_mats, offsets, precision=lax.Precision.HIGHEST
    )
    block_count = world_pos.shape[0] // 2
    return (
        world_pos.reshape(block_count, 2, 3, sub_count)
        .transpose(0, 2, 1, 3)
        .reshape(block_count, 3, 2 * sub_count)
    )


def contact(near_pos, far_pos):
    separation = near_pos[:, :, None] - far_pos[:, None, :]
    squared = jnp.sum(separation * separation, 0)
    weights = STIFFNESS * jnp.maximum(REACH_SQUARED - squared, 0.0)
    pushes = weights[None] * separation
    return (jnp.sum(pushes, 2), -jnp.sum(pushes, 1))


def anchor_moments(sphere_block, force_block):
    sub_count = sphere_block.shape[1] // 2
    spots = sphere_block.reshape(3, 2, sub_count)
    pushes = force_block.reshape(3, 2, sub_count)
    return jnp.concatenate([jnp.sum(pushes, -1), jnp.sum(cross_axis(spots, pushes), -1)], 0)


def shards(positions, rotations, clump_kind, sub_offsets, pair_blocks, pair_count):
    members = lax.axis_size("dev")
    group_index = lax.axis_index("grp")
    own_blocks = positions.shape[1] // 2
    group_blocks = own_blocks * members
    kind_count = sub_offsets.shape[0]
    sub_count = sub_offsets.shape[2]
    slot_group = 32
    offset_table = sub_offsets.astype(jnp.float32).reshape(kind_count, 3 * sub_count) * OFFSET_UNIT
    onehot = (clump_kind[:, None] == jnp.arange(kind_count, dtype=jnp.int32)[None, :]).astype(
        jnp.float32
    )
    own_spheres = place_blocks(positions, rotations, onehot, offset_table)
    gathered = lax.all_gather(own_spheres, "dev", axis=0, tiled=True)
    spheres = padded(gathered, (("grp", 0),), RIM)
    table_base = group_index * group_blocks - RIM
    first_local = pair_blocks[0] - table_base
    second_local = pair_blocks[1] - table_base
    live_count = pair_count[0]
    turn_count = (live_count + slot_group - 1) // slot_group
    table_rows = spheres.shape[0]
    zero_table = jnp.zeros((table_rows, 6, 2), jnp.float32)

    def visit_block(turn_index, totals):
        start_row = turn_index * slot_group
        first_block = lax.dynamic_slice_in_dim(first_local, start_row, slot_group, 0)
        second_block = lax.dynamic_slice_in_dim(second_local, start_row, slot_group, 0)
        live_part = (start_row + jnp.arange(slot_group, dtype=jnp.int32) < live_count).astype(
            jnp.float32
        )
        near_pos = spheres[first_block]
        far_pos = spheres[second_block]
        push_first, push_second = jax.vmap(contact)(near_pos, far_pos)
        weight_live = live_part[:, None, None]
        totals = totals.at[first_block].add(
            jax.vmap(anchor_moments)(near_pos, push_first) * weight_live
        )
        totals = totals.at[second_block].add(
            jax.vmap(anchor_moments)(far_pos, push_second) * weight_live
        )
        return totals

    totals = lax.fori_loop(0, turn_count, visit_block, zero_table)
    moments = totals.transpose(1, 0, 2).reshape(6, 2 * table_rows)
    rim_clumps = 2 * RIM
    rim_parts = jnp.concatenate(
        [moments[:, :rim_clumps], moments[:, moments.shape[1] - rim_clumps :]], 1
    )
    arrived = padded(rim_parts, (("grp", 1),), rim_clumps)
    interior = moments[:, rim_clumps : rim_clumps + 2 * group_blocks]
    interior = interior.at[:, :rim_clumps].add(arrived[:, :rim_clumps])
    interior = interior.at[:, interior.shape[1] - rim_clumps :].add(
        arrived[:, arrived.shape[1] - rim_clumps :]
    )
    summed = lax.psum_scatter(interior, "dev", scatter_dimension=1, tiled=True)
    clump_force = summed[0:3]
    clump_torque = summed[3:6] - cross_axis(positions, clump_force)
    return (clump_force, clump_torque)


def solution(mesh):
    placed = (
        P(None, ("grp", "dev")),
        P(None, ("grp", "dev")),
        P(("grp", "dev")),
        P(),
        P(None, ("grp", "dev")),
        P(("grp", "dev")),
    )
    return jax.shard_map(
        shards,
        mesh=mesh,
        in_specs=placed,
        out_specs=(P(None, ("grp", "dev")), P(None, ("grp", "dev"))),
        check_vma=False,
    )
```

profile of v0, /device:TPU:0, one launch (start us, length us, event | category | flops | bytes accessed | tf_op | source)
XLA Modules:
  0.0 1036.5 jit_solution(15804710355770445196)
XLA Ops:
  13.1 9.8 convolution_add_fusion
  26.1 100.9 %all-gather.2.cloned.1.call-done = f32[4096,3,128]{0,2,1:T(8,128)} async-done(((f32[512,3,128]{0,2,1:T(8,128)}), f32[4096,3,128]{0,2,1:T(8,128)}) %all-gather.2.cloned.1.call-update) | async-done | bytes 6291472 | tf_op jit(solution)/shard_map/all_gather | solution.py:85
  134.4 6.1 pad_maximum_fusion
  140.5 10.1 copy.151
  154.3 792.6 %while.12 = (s32[]{:T(128)}, f32[4352,6,2]{1,2,0:T(2,128)}, s32[]{:T(128)}, s32[1024]{0:T(1024)S(1)}, f32[4352,3,128]{2,1,0:T(4,128)}, /*index=5*/s32[1024]{0:T(...) while((s32[]{:T(128)}, f32[4352,6,2]{1,2,0:T(2,128)}, ...), condition=%wide.region_10.11_spmd, body=%wide.region_0.10_spmd.sunk | while | flops 12222438 | bytes 10249395 | solution.py:114
  154.3 4.1 gather_fusion
  158.5 4.1 gather_fusion.1
  179.1 4.1 gather_fusion
  183.3 4.1 gather_fusion.1
  203.8 4.1 gather_fusion
  208.0 4.1 gather_fusion.1
  232.7 4.1 gather_fusion.1
  253.3 4.1 gather_fusion
  257.4 4.1 gather_fusion.1
  278.1 4.1 gather_fusion
  282.2 4.1 gather_fusion.1
  302.9 4.1 gather_fusion
  307.1 4.1 gather_fusion.1
  327.8 4.1 gather_fusion
  331.9 4.1 gather_fusion.1
  352.5 4.1 gather_fusion
  356.7 4.1 gather_fusion.1
  377.2 4.1 gather_fusion
  381.4 4.1 gather_fusion.1
  402.0 4.1 gather_fusion
  406.2 4.1 gather_fusion.1
  426.8 4.1 gather_fusion
  430.9 4.1 gather_fusion.1
  455.8 4.1 gather_fusion.1
  476.3 4.1 gather_fusion
  480.4 4.1 gather_fusion.1
  501.0 4.1 gather_fusion
  505.2 4.1 gather_fusion.1
  525.7 4.1 gather_fusion
  529.9 4.1 gather_fusion.1
  550.5 4.1 gather_fusion
  554.7 4.1 gather_fusion.1
  575.3 4.1 gather_fusion
  579.5 4.1 gather_fusion.1
  600.0 4.1 gather_fusion
  604.1 4.1 gather_fusion.1
  628.9 4.1 gather_fusion.1
  649.6 4.1 gather_fusion
  653.7 4.1 gather_fusion.1
  678.5 4.1 gather_fusion.1
  703.3 4.1 gather_fusion.1
  723.9 4.1 gather_fusion
  728.1 4.1 gather_fusion.1
  748.7 4.1 gather_fusion
  752.8 4.1 gather_fusion.1
  773.4 4.1 gather_fusion
  802.4 4.1 gather_fusion.1
  823.1 4.1 gather_fusion
  827.3 4.1 gather_fusion.1
  847.8 4.1 gather_fusion
  852.0 4.1 gather_fusion.1
  872.6 4.1 gather_fusion
  876.8 4.1 gather_fusion.1
  897.3 4.1 gather_fusion
  901.5 4.1 gather_fusion.1
  922.2 4.1 gather_fusion
  926.3 4.1 gather_fusion.1
  949.9 4.4 slice.176
  961.1 66.2 %reduce-scatter.2.cloned.1.call-done = f32[6,1024]{1,0:T(8,128)} async-done(((f32[6,8192]{1,0:T(8,128)}), f32[6,1024]{1,0:T(8,128)}) %reduce-scatter.2.cloned.1.call-update) | async-done | bytes 24592 | tf_op jit(solution)/shard_map/reduce_scatter | solution.py:126
  (1040 shorter events, 583.4 us)
Async XLA Ops:
  7.2 5.7 copy-start.1
  7.2 119.8 %all-gather.2.cloned.1.call-start = ((), (), s32[]{:S(2)}) async-start(), calls=%async_computation.1 | async-start | bytes 7077888 | tf_op jit(solution)/shard_map/all_gather | solution.py:85
  13.1 117.6 %copy-start.2 = (s32[2,1024]{1,0:T(2,128)S(1)}, s32[2,1024]{1,0:T(2,128)}, u32[]{:S(2)}) copy-start(s32[2,1024]{1,0:T(2,128)} %param.16) | copy-start | bytes 24580
  25.4 1001.9 %reduce-scatter.2.cloned.1.call-start = ((), (), s32[]{:S(2)}) async-start(), calls=%async_computation.2 | async-start | bytes 294912 | tf_op jit(solution)/shard_map/reduce_scatter | solution.py:126
  128.0 2.6 collective-permute-start
  129.4 5.0 collective-permute-start.1
  948.0 10.6 %collective-permute-start.2 = (f32[6,256]{1,0:T(8,128)S(1)}, f32[6,256]{1,0:T(8,128)S(1)}, u32[]{:S(2)}, u32[]{:S(2)}) collective-permute-start(f32[6,256]{1,0:T(8,128)S(1)} %copy.158), channel_id=1, source_target_pairs={{0,8},{8,16},{16,24},{1,9},{9,17},{17,25},{2,10},{10,18},{18,26},{... | collective-permute-start | bytes 18440 | tf_op jit(solution)/shard_map/ppermute | solution.py:20
  957.3 3.1 collective-permute-start.3
  960.4 0.7 copy-start
Sparse Core Ops, SparseCore 0:
  25.5 101.4 all-gather.1
  961.2 66.0 reduce-scatter.1
where the time goes:
time: 1040 us
  other arithmetic  501 us (48%)
  local copies, waits for them, and re-layouts  328 us (32%)
  waiting for transfers between devices  172 us (17%)
  between operations  14.8 us (1%)
  matrix products  11 us (1%)
    gather x64, local copies, waits for them, and re-layouts, visit_block(): near_pos = spheres[first_block]  133 us
    gather x64, local copies, waits for them, and re-layouts, visit_block(): far_pos = spheres[second_block]  133 us
    reduce_sum x32, other arithmetic, contact(): return (jnp.sum(pushes, 2), -jnp.sum(pushes, 1))  130 us
    scatter-add x32, other arithmetic, visit_block(): totals.at[second_block]  116 us
    scatter-add x32, other arithmetic, visit_block(): totals.at[first_block]  115 us
    all_gather x1, waiting for transfers between devices, shards(): gathered = lax.all_gather(own_spheres, 'dev', axis=0, tiled=True)  101 us
    reduce_sum x32, other arithmetic, contact(): squared = jnp.sum(separation * separation, 0)  66.4 us
    reduce_scatter x1, waiting for transfers between devices, shards(): summed = lax.psum_scatter(interior, 'dev', scatter_dimension=1, tiled=True)  66.2 us
  transfers between devices with their start and end apart: 6, of which 4 were waited for; matrix products, arithmetic and copies ran while one was open for 1% of the time, Pallas kernels for 0%

commit v1 on v0

--- a/solution.py
+++ b/solution.py
@@ -82,7 +82,9 @@
         jnp.float32
     )
     own_spheres = place_blocks(positions, rotations, onehot, offset_table)
-    gathered = lax.all_gather(own_spheres, "dev", axis=0, tiled=True)
+    gathered = jnp.concatenate(
+        lax.all_to_all(jnp.stack([own_spheres] * lax.axis_size("dev")), "dev", 0, 0), axis=0
+    )
     spheres = padded(gathered, (("grp", 0),), RIM)
     table_base = group_index * group_blocks - RIM
     first_local = pair_blocks[0] - table_base

time: 1040 us -> 1100 us (1.058)
  waiting for transfers between devices: 172 us -> 209 us
  local copies, waits for them, and re-layouts: 328 us -> 343 us
    all_to_all x0 -> x1, waiting for transfers between devices: none -> 137 us  [shards(): lax.all_to_all(jnp.stack([own_spheres] * lax.axis_size('dev')), 'dev', 0, 0)]
    all_gather x1 -> x0, waiting for transfers between devices: 101 us -> none  [shards(): gathered = lax.all_gather(own_spheres, 'dev', axis=0, tiled=True)]
where the time goes in v1:
time: 1100 us; the launch traced here: 1090 us
  other arithmetic  495 us (45%)
  local copies, waits for them, and re-layouts  343 us (31%)
  waiting for transfers between devices  209 us (19%)
  between operations  14.9 us (1%)
  starting transfers between devices  12.5 us (1%)
    all_to_all x1, waiting for transfers between devices, shards(): lax.all_to_all(jnp.stack([own_spheres] * lax.axis_size('dev')), 'dev', 0, 0)  137 us
    gather x64, local copies, waits for them, and re-layouts, visit_block(): near_pos = spheres[first_block]  133 us
    gather x64, local copies, waits for them, and re-layouts, visit_block(): far_pos = spheres[second_block]  133 us
    reduce_sum x32, other arithmetic, contact(): return (jnp.sum(pushes, 2), -jnp.sum(pushes, 1))  130 us
    scatter-add x32, other arithmetic, visit_block(): totals.at[second_block]  116 us
    scatter-add x32, other arithmetic, visit_block(): totals.at[first_block]  115 us
    reduce_scatter x1, waiting for transfers between devices, shards(): summed = lax.psum_scatter(interior, 'dev', scatter_dimension=1, tiled=True)  67.2 us
    reduce_sum x32, other arithmetic, contact(): squared = jnp.sum(separation * separation, 0)  66.4 us
  transfers between devices with their start and end apart: 6, of which 4 were waited for; matrix products, arithmetic and copies ran while one was open for 1% of the time, Pallas kernels for 0%

profile of v1, /device:TPU:0, one launch (start us, length us, event | category | flops | bytes accessed | tf_op | source)
XLA Modules:
  0.0 1090.5 jit_solution(1485075344479039239)
XLA Ops:
  13.1 9.7 convolution_add_fusion
  28.2 7.3 all-to-all-start
  36.3 137.5 %all-to-all-done = f32[8,512,3,128]{3,1,2,0:T(8,128)} async-done(((f32[8,512,3,128]{3,1,2,0:T(8,128)}), f32[8,512,3,128]{3,1,2,0:T(8,128)}, u32[]{:S(2)}, u32[]{:S(2)}) %all-to-all-start) | async-done | bytes 6291488 | tf_op jit(solution)/shard_map/all_to_all | solution.py:86
  184.0 19.7 %copy.188 = f32[4352,3,128]{2,1,0:T(4,128)} copy(f32[4352,3,128]{2,0,1:T(8,128)S(1)} %pad_maximum_fusion) | data formatting | bytes 13369344 | tf_op jit(solution)/shard_map/while | solution.py:116
  207.3 792.6 %while.12 = (s32[]{:T(128)}, f32[4352,6,2]{1,2,0:T(2,128)}, s32[]{:T(128)}, s32[1024]{0:T(1024)S(1)}, f32[4352,3,128]{2,1,0:T(4,128)}, /*index=5*/s32[1024]{0:T(...) while((s32[]{:T(128)}, f32[4352,6,2]{1,2,0:T(2,128)}, ...), condition=%wide.region_10.11_spmd, body=%wide.region_0.10_spmd.sunk | while | flops 12222438 | bytes 10249395 | solution.py:116
  207.4 4.1 gather_fusion
  211.5 4.1 gather_fusion.1
  232.2 4.1 gather_fusion
  236.3 4.1 gather_fusion.1
  256.8 4.1 gather_fusion
  261.0 4.1 gather_fusion.1
  285.7 4.1 gather_fusion.1
  306.3 4.1 gather_fusion
  310.5 4.1 gather_fusion.1
  331.1 4.1 gather_fusion
  335.3 4.1 gather_fusion.1
  356.0 4.1 gather_fusion
  360.1 4.1 gather_fusion.1
  380.8 4.1 gather_fusion
  384.9 4.1 gather_fusion.1
  405.6 4.1 gather_fusion
  409.7 4.1 gather_fusion.1
  430.3 4.1 gather_fusion
  434.4 4.1 gather_fusion.1
  455.1 4.1 gather_fusion
  459.2 4.1 gather_fusion.1
  479.8 4.1 gather_fusion
  484.0 4.1 gather_fusion.1
  508.8 4.1 gather_fusion.1
  529.3 4.1 gather_fusion
  533.5 4.1 gather_fusion.1
  554.1 4.1 gather_fusion
  558.2 4.1 gather_fusion.1
  578.8 4.1 gather_fusion
  582.9 4.1 gather_fusion.1
  603.6 4.1 gather_fusion
  607.7 4.1 gather_fusion.1
  628.4 4.1 gather_fusion
  632.5 4.1 gather_fusion.1
  653.0 4.1 gather_fusion
  657.2 4.1 gather_fusion.1
  677.8 4.1 gather_fusion
  682.0 4.1 gather_fusion.1
  702.6 4.1 gather_fusion
  706.8 4.1 gather_fusion.1
  727.4 4.1 gather_fusion
  731.5 4.1 gather_fusion.1
  752.2 4.1 gather_fusion
  756.3 4.1 gather_fusion.1
  776.9 4.1 gather_fusion
  781.1 4.1 gather_fusion.1
  801.7 4.1 gather_fusion
  805.9 4.1 gather_fusion.1
  826.5 4.1 gather_fusion
  855.4 4.1 gather_fusion.1
  880.3 4.1 gather_fusion.1
  900.8 4.1 gather_fusion
  905.0 4.1 gather_fusion.1
  929.8 4.1 gather_fusion.1
  954.5 4.1 gather_fusion.1
  975.2 4.1 gather_fusion
  979.3 4.1 gather_fusion.1
  1002.9 4.4 slice.176
  1014.1 67.2 %reduce-scatter.2.cloned.1.call-done = f32[6,1024]{1,0:T(8,128)} async-done(((f32[6,8192]{1,0:T(8,128)}), f32[6,1024]{1,0:T(8,128)}) %reduce-scatter.2.cloned.1.call-update) | async-done | bytes 24592 | tf_op jit(solution)/shard_map/reduce_scatter | solution.py:128
  (1042 shorter events, 589.0 us)
Async XLA Ops:
  7.2 5.7 copy-start.1
  28.2 145.5 %all-to-all-start = ((f32[8,512,3,128]{3,1,2,0:T(8,128)}), f32[8,512,3,128]{3,1,2,0:T(8,128)}, u32[]{:S(2)}, u32[]{:S(2)}) async-start(f32[8,512,3,128]{3,1,2,0:T(8,128)} %stack.8), calls=%async_computation | async-start | bytes 12582912 | tf_op jit(solution)/shard_map/all_to_all | solution.py:86
  35.5 1045.7 %reduce-scatter.2.cloned.1.call-start = ((), (), s32[]{:S(2)}) async-start(), calls=%async_computation.2 | async-start | bytes 294912 | tf_op jit(solution)/shard_map/reduce_scatter | solution.py:128
  36.2 143.5 %copy-start.2 = (s32[2,1024]{1,0:T(2,128)S(1)}, s32[2,1024]{1,0:T(2,128)}, u32[]{:S(2)}) copy-start(s32[2,1024]{1,0:T(2,128)} %param.16) | copy-start | bytes 24580
  177.2 2.6 collective-permute-start
  178.5 5.1 collective-permute-start.1
  1001.0 10.6 collective-permute-start.2
  1010.3 3.1 collective-permute-start.3
  1013.4 0.7 copy-start
Sparse Core Ops, SparseCore 0:
  1014.2 66.9 reduce-scatter.1
